TPU v7x, 32 devices: a whole 2x2x4 slice. The times are simulated.
32 devices in a mesh: groups: 1, leaf: 32 (over z, y, x, core).
Axes of the slice: x: 2, y: 2, z: 4, core: 2. Of those that a mesh axis runs over, the one named last changes fastest.
Arguments:
- embeddings: bfloat16 [768, 65536], P(None, ('groups', 'leaf')), may hold values from -4 to 4
- probes: bfloat16 [32, 65536], P(None, ('groups', 'leaf')), may hold values from -1.75 to 1.75
- order: int32 [32, 2048], P(('groups', 'leaf')), may hold values from 0 to 2047, each once within a row
- near_list: int32 [256, 7], P(('groups', 'leaf')), may hold values from 0 to 255, as said below
- near_count: int32 [32, 8], P(('groups', 'leaf')), may hold values from 1 to 7, 32 in all within a row
- skeleton: int32 [30, 64], P('groups'), may hold values from 0 to 65535, as said below
- core: float32 [30, 64, 64], P('groups'), may hold values from -8 to 8
Outputs:
- values: float32 [32, 65536], P(None, ('groups', 'leaf'))
Inputs may be any that keep to these rules, and one draw needn't show every extreme that they name: `near_list`: slot 0 of leaf t holds t; every slot of leaf t holds a leaf within 3 of t. `near_count`: each row sums to 32, and its largest entry is 7. `skeleton`: entry r of node n lies among the examples of node n, in the r-th of 64 equal parts of them. `order`: each row is a permutation.
All inputs are finite; a program needn't handle non-finite values.
Results may differ from a plain program's by a relative error of at most 0.0042.
Values may be sent and summed in bfloat16 or wider, within the bound.
No kernel may reach another device: no remote copies, remote signals or barrier semaphores. Data moves between devices by JAX's collectives and lax.ppermute only.
A program may use at most 128 MiB of HBM per device.

v0:
```python
import jax
import jax.numpy as jnp
from jax import lax
from jax.sharding import PartitionSpec as P

LEAF = 256
R = 64
LEVELS = 4
W = 3
NEAR = 7


def with_halo(block, sides, width):
    for axis, dim in sides:
        count = lax.axis_size(axis)
        forward = [(i, i + 1) for i in range(count - 1)]
        backward = [(target, source) for source, target in forward]
        low = lax.ppermute(
            lax.slice_in_dim(block, block.shape[dim] - width, None, axis=dim), axis, forward
        )
        high = lax.ppermute(lax.slice_in_dim(block, 0, width, axis=dim), axis, backward)
        block = jnp.concatenate([low, block, high], axis=dim)
    return block


def kernel_matrix(left_emb, left_norm, right_emb, right_norm):
    inner = lax.dot_general(
        left_emb, right_emb, (((0,), (0,)), ((), ())), preferred_element_type=jnp.float32
    )
    distance = left_norm[:, None] + right_norm[None, :] - 2.0 * inner
    return jnp.exp(-0.5 * distance).astype(jnp.bfloat16)


def leaf_kernels(source_emb, source_norm, target_emb, target_norm):
    inner = jnp.einsum("eia,eib->iab", source_emb, target_emb, preferred_element_type=jnp.float32)
    distance = source_norm[:, :, None] + target_norm[:, None, :] - 2.0 * inner
    return jnp.exp(-0.5 * distance).astype(jnp.bfloat16)


def column_norms(columns):
    return jnp.sum(jnp.square(columns.astype(jnp.float32)), axis=0)


def body(embeddings, probes, order, near_list, near_count, skeleton, core):
    axis_devices = lax.axis_size("leaf")
    tree_bits = axis_devices.bit_length() - 1
    position = lax.axis_index("leaf")
    width_e = embeddings.shape[0]
    dev_points = embeddings.shape[1]
    dev_leaves = dev_points // LEAF
    x_tree = probes[:, order[0]]
    probe_cols = x_tree.shape[0]
    norms = column_norms(embeddings)
    stacked = jnp.concatenate([embeddings, x_tree], axis=0)
    padded = with_halo(stacked, (("leaf", 1),), W * LEAF)
    pad_blocks = padded.reshape(padded.shape[0], dev_leaves + 2 * W, LEAF)
    pad_emb = pad_blocks[:width_e]
    pad_x = pad_blocks[width_e:]
    pad_norm = jnp.sum(jnp.square(pad_emb.astype(jnp.float32)), axis=0)
    own_emb = embeddings.reshape(width_e, dev_leaves, LEAF)
    own_norm = norms.reshape(dev_leaves, LEAF)
    local_pos = near_list - position * dev_leaves + W
    counts = near_count[0]
    near_sum = jnp.zeros((probe_cols, dev_leaves, LEAF), jnp.float32)
    for slot_id in range(NEAR):
        sources = local_pos[:, slot_id]
        kernel_vals = leaf_kernels(
            jnp.take(pad_emb, sources, axis=1),
            jnp.take(pad_norm, sources, axis=0),
            own_emb,
            own_norm,
        )
        terms = jnp.einsum(
            "pia,iab->pib",
            jnp.take(pad_x, sources, axis=1),
            kernel_vals,
            preferred_element_type=jnp.float32,
        )
        near_sum = near_sum + jnp.where((slot_id < counts)[None, :, None], terms, 0.0)
    level_bits = [tree_bits - 1 - level_id for level_id in range(LEVELS)]
    own_nodes = [
        2 ** (level_id + 1) - 2 + jnp.right_shift(position, level_bits[level_id])
        for level_id in range(LEVELS)
    ]
    partner_nodes = [
        2 ** (level_id + 1)
        - 2
        + jnp.bitwise_xor(jnp.right_shift(position, level_bits[level_id]), 1)
        for level_id in range(LEVELS)
    ]
    start_point = position * dev_points
    slot_counts = [R * 2 ** (level_id + 1) // axis_devices for level_id in range(LEVELS)]
    slot_starts = [sum(slot_counts[:level_id]) for level_id in range(LEVELS)]
    picks = []
    for level_id in range(LEVELS):
        node_row = lax.dynamic_index_in_dim(skeleton, own_nodes[level_id], 0, keepdims=False)
        within = jnp.bitwise_and(position, (1 << level_bits[level_id]) - 1)
        point_ids = lax.dynamic_slice_in_dim(
            node_row, within * slot_counts[level_id], slot_counts[level_id]
        )
        picks.append(jnp.take(embeddings, point_ids - start_point, axis=1))
    owned = jnp.concatenate(picks, axis=1)
    gathered = lax.all_gather(owned, "leaf", axis=1, tiled=True)
    gathered = gathered.reshape(width_e, axis_devices, owned.shape[1])
    own_parts = []
    part_parts = []
    for level_id in range(LEVELS):
        first_node = 2 ** (level_id + 1) - 2
        level_cols = gathered[
            :, :, slot_starts[level_id] : slot_starts[level_id] + slot_counts[level_id]
        ]
        level_cols = level_cols.reshape(width_e, axis_devices * slot_counts[level_id])
        own_parts.append(
            lax.dynamic_slice_in_dim(level_cols, (own_nodes[level_id] - first_node) * R, R, axis=1)
        )
        part_parts.append(
            lax.dynamic_slice_in_dim(
                level_cols, (partner_nodes[level_id] - first_node) * R, R, axis=1
            )
        )
    own_cols = jnp.concatenate(own_parts, axis=1)
    part_cols = jnp.concatenate(part_parts, axis=1)
    own_sums = jnp.dot(
        x_tree,
        kernel_matrix(embeddings, norms, own_cols, column_norms(own_cols)),
        preferred_element_type=jnp.float32,
    )
    node_terms = jnp.zeros((probe_cols, skeleton.shape[0] * R), jnp.float32)
    for level_id in range(LEVELS):
        node_terms = lax.dynamic_update_slice_in_dim(
            node_terms,
            own_sums[:, level_id * R : (level_id + 1) * R],
            own_nodes[level_id] * R,
            axis=1,
        )
    node_totals = lax.psum(node_terms, "leaf")
    partner_sums = [
        lax.dynamic_slice_in_dim(node_totals, partner_nodes[level_id] * R, R, axis=1)
        for level_id in range(LEVELS)
    ]
    weights = []
    for level_id in range(LEVELS):
        core_part = lax.dynamic_index_in_dim(core, partner_nodes[level_id], 0, keepdims=False)
        weights.append(
            jnp.dot(partner_sums[level_id], core_part, precision=lax.Precision.HIGHEST).astype(
                jnp.bfloat16
            )
        )
    far_kernel = kernel_matrix(part_cols, column_norms(part_cols), embeddings, norms)
    far_sum = jnp.dot(
        jnp.concatenate(weights, axis=1), far_kernel, preferred_element_type=jnp.float32
    )
    tree_values = near_sum.reshape(probe_cols, dev_points) + far_sum
    return jnp.zeros_like(tree_values).at[:, order[0]].set(tree_values)


def solution(mesh):
    return jax.shard_map(
        body,
        mesh=mesh,
        in_specs=(
            P(None, ("groups", "leaf")),
            P(None, ("groups", "leaf")),
            P(("groups", "leaf"), None),
            P(("groups", "leaf"), None),
            P(("groups", "leaf"), None),
            P("groups", None),
            P("groups", None, None),
        ),
        out_specs=P(None, ("groups", "leaf")),
        check_vma=False,
    )
```

profile of v0, /device:TPU:0, one launch (start us, length us, event | category | flops | bytes accessed | tf_op | source)
XLA Modules:
  0.0 336.7 jit_solution(11105078149921155437)
XLA Ops:
  10.7 4.6 %copy.41 = bf16[768,2048]{0,1:T(8,128)(2,1)} copy(bf16[768,2048]{1,0:T(8,128)(2,1)} %param.13) | data formatting | bytes 6291456 | tf_op args[0]
  15.4 2.9 gather_fusion.1
  18.3 2.9 gather_fusion.2
  21.2 2.9 gather_fusion.3
  24.1 2.9 gather_fusion.4
  28.4 6.2 %gather_fusion = bf16[2048,32]{1,0:T(8,128)(2,1)S(1)} fusion(bf16[32,2048]{0,1:T(8,128)(2,1)S(1)} %copy.40, s32[2048]{0:T(1024)S(1)} %broadcast_clamp_fusion), kind=kCustom, calls=%fused_computation.21 | custom fusion | bytes 270336 | tf_op jit(solution)/shard_map/gather | solution.py:51
  34.6 3.0 pad_maximum_fusion.4
  43.0 4.2 %collective-permute-start = (bf16[800,768]{1,0:T(8,128)(2,1)}, bf16[800,768]{1,0:T(8,128)(2,1)}, u32[]{:S(2)}, u32[]{:S(2)}) collective-permute-start(bf16[800,768]{1,0:T(8,128)(2,1)} %copy.42), channel_id=1, source_target_pairs={{0,1},{1,2},{2,3},{3,4},{4,5},{5,6},{6,7},{7,8},{8,9},{9,10},{10,1... | collective-permute-start | bytes 3686408 | tf_op jit(solution)/shard_map/ppermute | solution.py:18
  47.2 2.6 multiply_reduce_fusion.1
  54.3 6.6 %multiply_reduce_fusion = (f32[3584]{0:T(1024)S(1)}, bf16[768,3584]{0,1:T(8,128)(2,1)}) fusion(bf16[800,768]{0,1:T(8,128)(2,1)S(1)} %copy.45, bf16[32,2048]{0,1:T(8,128)(2,1)S(1)} %bitcast.279, bf16[768,2048]{0,1:T(8,128)(2,1)} %copy.41, bf16[800,768]{0,1:T(8,128)(2,1)} %copy.44), kind=kLoop, calls=%fused_computation.27 | loop fusion | flops 30274048 | bytes 11253760 | tf_op jit(solution)/shard_map/reduce_sum | solution.py:59
  72.5 8.2 %copy.46 = bf16[768,14,256]{2,0,1:T(8,128)(2,1)} copy(bf16[768,14,256]{0,2,1:T(8,128)(2,1)} %bitcast.269) | data formatting | bytes 11010048 | tf_op jit(solution)/shard_map/slice | solution.py:57
  80.7 5.1 %gather_fusion.6 = bf16[8,768,256]{2,1,0:T(8,128)(2,1)} fusion(bf16[768,14,256]{2,0,1:T(8,128)(2,1)} %copy.46, s32[1024]{0:T(1024)S(1)} %pad_clamp_fusion.10), kind=kCustom, calls=%fused_computation.1.clone | custom fusion | bytes 6291488 | tf_op jit(solution)/shard_map/jit(_take)/gather | solution.py:68
  85.7 5.0 %gather_fusion.9 = bf16[8,768,256]{2,1,0:T(8,128)(2,1)} fusion(bf16[768,14,256]{2,0,1:T(8,128)(2,1)} %copy.46, s32[1024]{0:T(1024)S(1)} %pad_clamp_fusion.9), kind=kCustom, calls=%fused_computation.9.clone | custom fusion | bytes 6291488 | tf_op jit(solution)/shard_map/jit(_take)/gather | solution.py:68
  90.7 5.0 %gather_fusion.12 = bf16[8,768,256]{2,1,0:T(8,128)(2,1)} fusion(bf16[768,14,256]{2,0,1:T(8,128)(2,1)} %copy.46, s32[1024]{0:T(1024)S(1)} %pad_clamp_fusion.8), kind=kCustom, calls=%fused_computation.10.clone | custom fusion | bytes 6291488 | tf_op jit(solution)/shard_map/jit(_take)/gather | solution.py:68
  95.6 5.0 %gather_fusion.15 = bf16[8,768,256]{2,1,0:T(8,128)(2,1)} fusion(bf16[768,14,256]{2,0,1:T(8,128)(2,1)} %copy.46, s32[1024]{0:T(1024)S(1)} %pad_clamp_fusion.7), kind=kCustom, calls=%fused_computation.11.clone | custom fusion | bytes 6291488 | tf_op jit(solution)/shard_map/jit(_take)/gather | solution.py:68
  100.6 5.0 %gather_fusion.18 = bf16[8,768,256]{2,1,0:T(8,128)(2,1)} fusion(bf16[768,14,256]{2,0,1:T(8,128)(2,1)} %copy.46, s32[1024]{0:T(1024)S(1)} %pad_clamp_fusion.6), kind=kCustom, calls=%fused_computation.12.clone | custom fusion | bytes 6291488 | tf_op jit(solution)/shard_map/jit(_take)/gather | solution.py:68
  105.7 5.1 %gather_fusion.21 = bf16[8,768,256]{2,1,0:T(8,128)(2,1)} fusion(bf16[768,14,256]{2,0,1:T(8,128)(2,1)} %copy.46, s32[1024]{0:T(1024)S(1)} %pad_clamp_fusion.5), kind=kCustom, calls=%fused_computation.13.clone | custom fusion | bytes 6291488 | tf_op jit(solution)/shard_map/jit(_take)/gather | solution.py:68
  110.8 5.0 %gather_fusion.24 = bf16[8,768,256]{2,1,0:T(8,128)(2,1)} fusion(bf16[768,14,256]{2,0,1:T(8,128)(2,1)} %copy.46, s32[1024]{0:T(1024)S(1)} %pad_clamp_fusion.4), kind=kCustom, calls=%fused_computation.14.clone | custom fusion | bytes 6291488 | tf_op jit(solution)/shard_map/jit(_take)/gather | solution.py:68
  116.2 3.9 %fusion.181 = f32[8,256,32]{1,2,0:T(8,128)S(1)} fusion(bf16[8,768,256]{2,1,0:T(8,128)(2,1)} %gather_fusion.6, pred[8]{0:T(512)(128)(4,1)S(1)} %get-tuple-element.58, f32[8,256]{1,0:T(8,128)S(1)} %add.373, f32[8,256]{1,0:T(8,128)S(1)} %broadcast_select_fusion.6, bf16[96,8,8,256]{3,2,1,0:T(8,128)(2,1)} %bitcast.270, ...), kind=kOutput, calls=%fused_computation.117 | convolution fusion | flops 843186176 | bytes 6701072 | tf_op jit(solution)/shard_map/pia,iab->pib/dot_general | solution.py:73
  120.1 3.9 %fusion.176 = f32[8,256,32]{1,2,0:T(8,128)S(1)} fusion(f32[8,256,32]{1,2,0:T(8,128)S(1)} %fusion.181, bf16[8,768,256]{2,1,0:T(8,128)(2,1)} %gather_fusion.9, pred[8]{0:T(512)(128)(4,1)S(1)} %get-tuple-element.57, f32[8,256]{1,0:T(8,128)S(1)} %broadcast_select_fusion.5, f32[8,256]{1,0:T(8,128)S(1)} %add.373, bf16[96,8,8,256]{3,2,1,0:T(8,128)(2,1)} %bitcast.271, ...), kind=kOutput, calls=%fused_computation.116 | convolution fusion | flops 843251712 | bytes 6963216 | tf_op jit(solution)/shard_map/pia,iab->pib/dot_general | solution.py:73
  124.0 3.9 %fusion.166 = f32[8,256,32]{1,2,0:T(8,128)S(1)} fusion(f32[8,256,32]{1,2,0:T(8,128)S(1)} %fusion.176, bf16[8,768,256]{2,1,0:T(8,128)(2,1)} %gather_fusion.12, pred[8]{0:T(512)(128)(4,1)S(1)} %get-tuple-element.56, f32[8,256]{1,0:T(8,128)S(1)} %broadcast_select_fusion.4, f32[8,256]{1,0:T(8,128)S(1)} %add.373, bf16[96,8,8,256]{3,2,1,0:T(8,128)(2,1)} %bitcast.272, ...), kind=kOutput, calls=%fused_computation.114 | convolution fusion | flops 843251712 | bytes 6963216 | tf_op jit(solution)/shard_map/pia,iab->pib/dot_general | solution.py:73
  127.9 3.9 %fusion.156 = f32[8,256,32]{1,2,0:T(8,128)S(1)} fusion(f32[8,256,32]{1,2,0:T(8,128)S(1)} %fusion.166, bf16[8,768,256]{2,1,0:T(8,128)(2,1)} %gather_fusion.15, pred[8]{0:T(512)(128)(4,1)S(1)} %get-tuple-element.55, f32[8,256]{1,0:T(8,128)S(1)} %broadcast_select_fusion.3, f32[8,256]{1,0:T(8,128)S(1)} %add.373, bf16[96,8,8,256]{3,2,1,0:T(8,128)(2,1)} %bitcast.273, ...), kind=kOutput, calls=%fused_computation.112 | convolution fusion | flops 843251712 | bytes 6963216 | tf_op jit(solution)/shard_map/pia,iab->pib/dot_general | solution.py:73
  131.8 3.9 %fusion.146 = f32[8,256,32]{1,2,0:T(8,128)S(1)} fusion(f32[8,256,32]{1,2,0:T(8,128)S(1)} %fusion.156, bf16[8,768,256]{2,1,0:T(8,128)(2,1)} %gather_fusion.18, pred[8]{0:T(512)(128)(4,1)S(1)} %get-tuple-element.54, f32[8,256]{1,0:T(8,128)S(1)} %broadcast_select_fusion.2, f32[8,256]{1,0:T(8,128)S(1)} %add.373, bf16[96,8,8,256]{3,2,1,0:T(8,128)(2,1)} %bitcast.274, ...), kind=kOutput, calls=%fused_computation.110 | convolution fusion | flops 843251712 | bytes 6963216 | tf_op jit(solution)/shard_map/pia,iab->pib/dot_general | solution.py:73
  135.7 5.2 %fusion.136 = f32[8,256,32]{1,2,0:T(8,128)} fusion(f32[8,256,32]{1,2,0:T(8,128)S(1)} %fusion.146, bf16[8,768,256]{2,1,0:T(8,128)(2,1)} %gather_fusion.21, pred[8]{0:T(512)(128)(4,1)S(1)} %get-tuple-element.53, f32[8,256]{1,0:T(8,128)S(1)} %broadcast_select_fusion.1, f32[8,256]{1,0:T(8,128)S(1)} %add.373, bf16[96,8,8,256]{3,2,1,0:T(8,128)(2,1)} %bitcast.275, ...), kind=kOutput, calls=%fused_computation.108 | convolution fusion | flops 843251712 | bytes 6963216 | tf_op jit(solution)/shard_map/pia,iab->pib/dot_general | solution.py:73
  140.9 5.3 %reshape.494 = bf16[1920,768]{1,0:T(8,128)(2,1)} reshape(bf16[32,60,768]{2,1,0:T(8,128)(2,1)} %all-gather.3.cloned.1.call-done) | data formatting | bytes 5898240
  146.2 5.3 %reshape.251 = bf16[768,32,60]{0,2,1:T(8,128)(2,1)} reshape(bf16[768,1920]{0,1:T(8,128)(2,1)} %bitcast.277) | data formatting | bytes 5898240 | tf_op jit(solution)/shard_map/reshape | solution.py:104
  155.4 3.4 %slice.139 = bf16[768,32,32]{0,2,1:T(8,128)(2,1)} slice(bf16[768,32,60]{0,2,1:T(8,128)(2,1)} %reshape.251), slice={[0:768], [0:32], [28:60]} | slice | bytes 3145728 | tf_op jit(solution)/shard_map/slice | solution.py:109
  160.1 3.3 fusion.52
  165.7 3.9 %fusion.126 = f32[8,4,8,256]{3,2,1,0:T(8,128)S(1)} fusion(f32[8,256,32]{1,2,0:T(8,128)S(1)} %copy-done.5, bf16[8,768,256]{2,1,0:T(8,128)(2,1)} %gather_fusion.24, pred[8]{0:T(512)(128)(4,1)S(1)} %get-tuple-element.52, f32[8,256]{1,0:T(8,128)S(1)} %broadcast_select_fusion, f32[8,256]{1,0:T(8,128)S(1)} %add.373, bf16[96,8,8,256]{3,2,1,0:T(8,128)(2,1)} %bitcast.276, ...), kind=kOutput, calls=%fused_computation.106 | convolution fusion | flops 843251712 | bytes 6963216 | tf_op jit(solution)/shard_map/pia,iab->pib/dot_general | solution.py:73
  169.8 145.9 %all-reduce.2.cloned.1.call-done = f32[32,1920]{1,0:T(8,128)} async-done(((f32[32,1920]{1,0:T(8,128)}), f32[32,1920]{1,0:T(8,128)}) %all-reduce.2.cloned.1.call-update) | async-done | bytes 245776 | tf_op jit(solution)/shard_map/psum | solution.py:136
  319.4 3.2 fusion.44
  323.0 5.8 %scatter_custom_fusion = f32[32,2048]{0,1:T(8,128)S(1)} fusion(s32[2048]{0:T(1024)S(1)} %bitcast.286, f32[2048,32]{1,0:T(8,128)S(1)} %copy.80, f32[]{:T(128)} %constant.201.clone.1), kind=kCustom, calls=%fused_computation.168 | custom fusion | bytes 262148 | tf_op jit(solution)/shard_map/scatter | solution.py:154
  (109 shorter events, 39.7 us)
Async XLA Ops:
  6.5 309.1 %copy-start = (f32[30,64,64]{2,1,0:T(8,128)S(1)}, f32[30,64,64]{2,1,0:T(8,128)}, u32[]{:S(2)}) copy-start(f32[30,64,64]{2,1,0:T(8,128)} %param.19) | copy-start | bytes 1474564
  6.5 134.4 %all-gather.3.cloned.1.call-start = ((), (), s32[]{:S(2)}) async-start(), calls=%async_computation.1 | async-start | bytes 3244032 | tf_op jit(solution)/shard_map/all_gather | solution.py:103
  18.2 9.8 %copy-start.3 = (s32[1,2048]{1,0:T(1,128)S(1)}, s32[1,2048]{1,0:T(1,128)}, u32[]{:S(2)}) copy-start(s32[1,2048]{1,0:T(1,128)} %param.15) | copy-start | bytes 24580
  18.3 9.9 %copy-start.2 = (bf16[32,2048]{1,0:T(8,128)(2,1)S(1)}, bf16[32,2048]{1,0:T(8,128)(2,1)}, u32[]{:S(2)}) copy-start(bf16[32,2048]{1,0:T(8,128)(2,1)} %param.14) | copy-start | bytes 393220
  28.0 287.6 %all-reduce.2.cloned.1.call-start = ((), (), s32[]{:S(2)}) async-start(), calls=%async_computation | async-start | bytes 491520 | tf_op jit(solution)/shard_map/psum | solution.py:136
  40.1 9.9 %copy-start.4 = (s32[1,8]{1,0:T(1,128)S(1)}, s32[1,8]{1,0:T(1,128)}, u32[]{:S(2)}) copy-start(s32[1,8]{1,0:T(1,128)} %param.17) | copy-start | bytes 100
  40.1 10.0 %collective-permute-start.1 = (bf16[800,768]{1,0:T(8,128)(2,1)}, bf16[800,768]{1,0:T(8,128)(2,1)}, u32[]{:S(2)}, u32[]{:S(2)}) collective-permute-start(bf16[800,768]{1,0:T(8,128)(2,1)} %copy.43), channel_id=1, source_target_pairs={{1,0},{2,1},{3,2},{4,3},{5,4},{6,5},{7,6},{8,7},{9,8},{10,9},{11,1... | collective-permute-start | bytes 3686408 | tf_op jit(solution)/shard_map/ppermute | solution.py:21
  43.0 8.8 %collective-permute-start = (bf16[800,768]{1,0:T(8,128)(2,1)}, bf16[800,768]{1,0:T(8,128)(2,1)}, u32[]{:S(2)}, u32[]{:S(2)}) collective-permute-start(bf16[800,768]{1,0:T(8,128)(2,1)} %copy.42), channel_id=1, source_target_pairs={{0,1},{1,2},{2,3},{3,4},{4,5},{5,6},{6,7},{7,8},{8,9},{9,10},{10,1... | collective-permute-start | bytes 3686408 | tf_op jit(solution)/shard_map/ppermute | solution.py:18
  160.1 5.6 %copy-start.5 = (f32[8,256,32]{1,2,0:T(8,128)S(1)}, f32[8,256,32]{1,2,0:T(8,128)}, u32[]{:S(2)}) copy-start(f32[8,256,32]{1,2,0:T(8,128)} %fusion.136) | copy-start | bytes 786436
  165.0 0.7 copy-start.1
Sparse Core Ops, SparseCore 0:
  28.2 68.4 all-gather.2
  165.8 149.8 all-reduce.1
where the time goes:
time: 339 us; the launch traced here: 337 us
  waiting for transfers between devices  146 us (43%)
  local copies, waits for them, and re-layouts  112 us (33%)
  matrix products  38.8 us (11%)
  other arithmetic  20.1 us (6%)
  between operations  14 us (4%)
  starting transfers between devices  5.62 us (2%)
    psum x1, waiting for transfers between devices, body(): node_totals = lax.psum(node_terms, 'leaf')  146 us
    gather x7, local copies, waits for them, and re-layouts, body(): jnp.take(pad_emb, sources, axis=1)  35.1 us
    dot_general x7, matrix products, body(): jnp.einsum('pia,iab->pib', jnp.take(pad_x, sources, axis=1), kernel_vals,...  28.6 us
    gather x4, local copies, waits for them, and re-layouts, body(): picks.append(jnp.take(embeddings, point_ids - start_point, axis=1))  11.6 us
    unnamed x15, local copies, waits for them, and re-layouts  10.9 us
    slice x1, local copies, waits for them, and re-layouts, body(): pad_emb = pad_blocks[:width_e]  8.19 us
    scatter x2, local copies, waits for them, and re-layouts, body(): return jnp.zeros_like(tree_values).at[:, order[0]].set(tree_values)  6.86 us
  transfers between devices with their start and end apart: 4, of which 1 were waited for; matrix products, arithmetic and copies ran while one was open for 33% of the time, Pallas kernels for 0%

commit v1 on v0

--- a/solution.py
+++ b/solution.py
@@ -133,7 +133,11 @@
             own_nodes[level_id] * R,
             axis=1,
         )
-    node_totals = lax.psum(node_terms, "leaf")
+    node_totals = node_terms
+    for hop in (1, 2, 4, 8, 16):
+        node_totals = node_totals + lax.ppermute(
+            node_totals, "leaf", [(dev, dev ^ hop) for dev in range(32)]
+        )
     partner_sums = [
         lax.dynamic_slice_in_dim(node_totals, partner_nodes[level_id] * R, R, axis=1)
         for level_id in range(LEVELS)

time: 339 us -> 231 us (0.68)
  waiting for transfers between devices: 146 us -> 7.19 us
  starting transfers between devices: 5.62 us -> 37 us
    psum x1 -> x0, waiting for transfers between devices: 146 us -> none  [body(): node_totals = lax.psum(node_terms, 'leaf')]
    ppermute x0 -> x5, starting transfers between devices: none -> 31.4 us  [body(): lax.ppermute(node_totals, 'leaf', [(dev, dev ^ hop) for dev in range(32)])]
    ppermute x0 -> x5, waiting for transfers between devices: none -> 7.16 us  [body(): lax.ppermute(node_totals, 'leaf', [(dev, dev ^ hop) for dev in range(32)])]
    unnamed x15 -> x23, local copies, waits for them, and re-layouts: 10.9 us -> 10.3 us
  transfers between devices with their start and end apart: 4 -> 8, of which waited for: 1 -> 1; matrix products, arithmetic and copies ran while one was open for 33% -> 50% of each run, Pallas kernels for 0% -> 0%
where the time goes in v1:
time: 231 us; the launch traced here: 230 us
  local copies, waits for them, and re-layouts  113 us (49%)
  matrix products  38 us (16%)
  starting transfers between devices  37 us (16%)
  other arithmetic  20.9 us (9%)
  between operations  14.1 us (6%)
  waiting for transfers between devices  7.19 us (3%)
    gather x7, local copies, waits for them, and re-layouts, body(): jnp.take(pad_emb, sources, axis=1)  35.1 us
    ppermute x5, starting transfers between devices, body(): lax.ppermute(node_totals, 'leaf', [(dev, dev ^ hop) for dev in range(32)])  31.4 us
    dot_general x7, matrix products, body(): jnp.einsum('pia,iab->pib', jnp.take(pad_x, sources, axis=1), kernel_vals,...  30.6 us
    gather x4, local copies, waits for them, and re-layouts, body(): picks.append(jnp.take(embeddings, point_ids - start_point, axis=1))  11.6 us
    unnamed x23, local copies, waits for them, and re-layouts  10.3 us
    slice x1, local copies, waits for them, and re-layouts, body(): pad_emb = pad_blocks[:width_e]  8.35 us
    ppermute x5, waiting for transfers between devices, body(): lax.ppermute(node_totals, 'leaf', [(dev, dev ^ hop) for dev in range(32)])  7.16 us
    scatter x2, local copies, waits for them, and re-layouts, body(): return jnp.zeros_like(tree_values).at[:, order[0]].set(tree_values)  6.86 us
  transfers between devices with their start and end apart: 8, of which 1 were waited for; matrix products, arithmetic and copies ran while one was open for 50% of the time, Pallas kernels for 0%

profile of v1, /device:TPU:0, one launch (start us, length us, event | category | flops | bytes accessed | tf_op | source)
XLA Modules:
  0.0 229.7 jit_solution(8790298075548837812)
XLA Ops:
  10.7 4.7 %copy.41 = bf16[768,2048]{0,1:T(8,128)(2,1)} copy(bf16[768,2048]{1,0:T(8,128)(2,1)} %param.13) | data formatting | bytes 6291456 | tf_op args[0]
  15.4 2.9 %gather_fusion.1 = bf16[4,768]{1,0:T(4,128)(2,1)S(1)} fusion(bf16[768,2048]{0,1:T(8,128)(2,1)} %copy.41, s32[1024]{0:T(1024)S(1)} %pad_clamp_fusion.3), kind=kCustom, calls=%fused_computation.22 | custom fusion | bytes 12304 | tf_op jit(solution)/shard_map/jit(_take)/gather | solution.py:101
  18.3 2.9 %gather_fusion.2 = bf16[8,768]{1,0:T(8,128)(2,1)S(1)} fusion(bf16[768,2048]{0,1:T(8,128)(2,1)} %copy.41, s32[1024]{0:T(1024)S(1)} %pad_clamp_fusion.2), kind=kCustom, calls=%fused_computation.23 | custom fusion | bytes 24608 | tf_op jit(solution)/shard_map/jit(_take)/gather | solution.py:101
  21.2 2.9 %gather_fusion.3 = bf16[16,768]{1,0:T(8,128)(2,1)S(1)} fusion(bf16[768,2048]{0,1:T(8,128)(2,1)} %copy.41, s32[1024]{0:T(1024)S(1)} %pad_clamp_fusion.1), kind=kCustom, calls=%fused_computation.24 | custom fusion | bytes 49216 | tf_op jit(solution)/shard_map/jit(_take)/gather | solution.py:101
  24.1 2.9 %gather_fusion.4 = bf16[32,768]{1,0:T(8,128)(2,1)S(1)} fusion(bf16[768,2048]{0,1:T(8,128)(2,1)} %copy.41, s32[1024]{0:T(1024)S(1)} %pad_clamp_fusion), kind=kCustom, calls=%fused_computation.25 | custom fusion | bytes 98432 | tf_op jit(solution)/shard_map/jit(_take)/gather | solution.py:101
  28.4 6.2 %gather_fusion = bf16[2048,32]{1,0:T(8,128)(2,1)S(1)} fusion(bf16[32,2048]{0,1:T(8,128)(2,1)S(1)} %copy.40, s32[2048]{0:T(1024)S(1)} %broadcast_clamp_fusion), kind=kCustom, calls=%fused_computation.21 | custom fusion | bytes 270336 | tf_op jit(solution)/shard_map/gather | solution.py:51
  34.6 3.0 %pad_maximum_fusion.4 = (bf16[800,768]{0,1:T(8,128)(2,1)S(1)}, bf16[800,768]{0,1:T(8,128)(2,1)}) fusion(bf16[32,2048]{0,1:T(8,128)(2,1)S(1)} %bitcast.278, bf16[768,2048]{0,1:T(8,128)(2,1)} %copy.41), kind=kLoop, calls=%fused_computation.95 | loop fusion | flops 4915200 | bytes 5734400 | tf_op jit(solution)/shard_map/slice | solution.py:19
  43.0 4.2 %collective-permute-start = (bf16[800,768]{1,0:T(8,128)(2,1)}, bf16[800,768]{1,0:T(8,128)(2,1)}, u32[]{:S(2)}, u32[]{:S(2)}) collective-permute-start(bf16[800,768]{1,0:T(8,128)(2,1)} %copy.42), channel_id=1, source_target_pairs={{0,1},{1,2},{2,3},{3,4},{4,5},{5,6},{6,7},{7,8},{8,9},{9,10},{10,1... | collective-permute-start | bytes 3686408 | tf_op jit(solution)/shard_map/ppermute | solution.py:18
  55.0 6.8 %multiply_reduce_fusion = (f32[3584]{0:T(1024)S(1)}, bf16[768,3584]{0,1:T(8,128)(2,1)}) fusion(bf16[800,768]{0,1:T(8,128)(2,1)S(1)} %copy.45, bf16[32,2048]{0,1:T(8,128)(2,1)S(1)} %bitcast.279, bf16[768,2048]{0,1:T(8,128)(2,1)} %copy.41, bf16[800,768]{0,1:T(8,128)(2,1)} %copy.44), kind=kLoop, calls=%fused_computation.27 | loop fusion | flops 30274048 | bytes 11253760 | tf_op jit(solution)/shard_map/reduce_sum | solution.py:59
  69.4 8.4 %copy.46 = bf16[768,14,256]{2,0,1:T(8,128)(2,1)} copy(bf16[768,14,256]{0,2,1:T(8,128)(2,1)} %bitcast.269) | data formatting | bytes 11010048 | tf_op jit(solution)/shard_map/slice | solution.py:57
  77.7 5.3 %gather_fusion.6 = bf16[8,768,256]{2,1,0:T(8,128)(2,1)} fusion(bf16[768,14,256]{2,0,1:T(8,128)(2,1)} %copy.46, s32[1024]{0:T(1024)S(1)} %pad_clamp_fusion.10), kind=kCustom, calls=%fused_computation.1.clone | custom fusion | bytes 6291488 | tf_op jit(solution)/shard_map/jit(_take)/gather | solution.py:68
  83.0 5.0 %gather_fusion.9 = bf16[8,768,256]{2,1,0:T(8,128)(2,1)} fusion(bf16[768,14,256]{2,0,1:T(8,128)(2,1)} %copy.46, s32[1024]{0:T(1024)S(1)} %pad_clamp_fusion.9), kind=kCustom, calls=%fused_computation.9.clone | custom fusion | bytes 6291488 | tf_op jit(solution)/shard_map/jit(_take)/gather | solution.py:68
  88.0 5.0 %gather_fusion.12 = bf16[8,768,256]{2,1,0:T(8,128)(2,1)} fusion(bf16[768,14,256]{2,0,1:T(8,128)(2,1)} %copy.46, s32[1024]{0:T(1024)S(1)} %pad_clamp_fusion.8), kind=kCustom, calls=%fused_computation.10.clone | custom fusion | bytes 6291488 | tf_op jit(solution)/shard_map/jit(_take)/gather | solution.py:68
  93.2 4.0 %fusion.181 = f32[8,256,32]{1,2,0:T(8,128)S(1)} fusion(bf16[8,768,256]{2,1,0:T(8,128)(2,1)} %gather_fusion.6, pred[8]{0:T(512)(128)(4,1)S(1)} %get-tuple-element.58, f32[8,256]{1,0:T(8,128)S(1)} %add.386, f32[8,256]{1,0:T(8,128)S(1)} %broadcast_select_fusion.6, bf16[96,8,8,256]{3,2,1,0:T(8,128)(2,1)} %bitcast.270, ...), kind=kOutput, calls=%fused_computation.117 | convolution fusion | flops 843186176 | bytes 6701072 | tf_op jit(solution)/shard_map/pia,iab->pib/dot_general | solution.py:73
  97.2 5.2 %fusion.176 = f32[8,256,32]{1,2,0:T(8,128)} fusion(f32[8,256,32]{1,2,0:T(8,128)S(1)} %fusion.181, bf16[8,768,256]{2,1,0:T(8,128)(2,1)} %gather_fusion.9, pred[8]{0:T(512)(128)(4,1)S(1)} %get-tuple-element.57, f32[8,256]{1,0:T(8,128)S(1)} %broadcast_select_fusion.5, f32[8,256]{1,0:T(8,128)S(1)} %add.386, bf16[96,8,8,256]{3,2,1,0:T(8,128)(2,1)} %bitcast.271, ...), kind=kOutput, calls=%fused_computation.116 | convolution fusion | flops 843251712 | bytes 6963216 | tf_op jit(solution)/shard_map/pia,iab->pib/dot_general | solution.py:73
  102.4 5.3 %reshape.494 = bf16[1920,768]{1,0:T(8,128)(2,1)} reshape(bf16[32,60,768]{2,1,0:T(8,128)(2,1)} %all-gather.3.cloned.1.call-done) | data formatting | bytes 5898240
  107.7 5.3 %reshape.251 = bf16[768,32,60]{0,2,1:T(8,128)(2,1)} reshape(bf16[768,1920]{0,1:T(8,128)(2,1)} %bitcast.277) | data formatting | bytes 5898240 | tf_op jit(solution)/shard_map/reshape | solution.py:104
  116.8 3.5 %slice.139 = bf16[768,32,32]{0,2,1:T(8,128)(2,1)} slice(bf16[768,32,60]{0,2,1:T(8,128)(2,1)} %reshape.251), slice={[0:768], [0:32], [28:60]} | slice | bytes 3145728 | tf_op jit(solution)/shard_map/slice | solution.py:109
  121.6 3.3 %fusion.52 = f32[32,256]{1,0:T(8,128)S(1)} fusion(bf16[2048,32]{1,0:T(8,128)(2,1)S(1)} %gather_fusion, bf16[768,2048]{1,0:T(8,128)(2,1)} %param.13, f32[256]{0:T(256)S(1)} %multiply_reduce_fusion.3, f32[2048]{0:T(1024)S(1)} %multiply_reduce_fusion.1, bf16[768,64]{0,1:T(8,128)(2,1)S(1)} %get-tuple-element.27, bf16[768,64]{0,1:T(8,128)(2,1)S(1)} %get-tuple-element.29, ...), kind=kOutput, calls=%fused_computation.96 | convolution fusion | flops 843055104 | bytes 3712000 | tf_op jit(solution)/shard_map/dot_general | solution.py:123
  126.5 24.5 %collective-permute-start.2 = (f32[32,1920]{1,0:T(8,128)S(1)}, f32[32,1920]{1,0:T(8,128)S(1)}, u32[]{:S(2)}, u32[]{:S(2)}) collective-permute-start(f32[32,1920]{1,0:T(8,128)S(1)} %dynamic_update_slice.15), channel_id=1, source_target_pairs={{0,1},{1,0},{2,3},{3,2},{4,5},{5,4},{6,7},{7,6},{8,9},{9,8},{10,11... | collective-permute-start | bytes 737288 | tf_op jit(solution)/shard_map/ppermute | solution.py:138
  151.0 4.5 %fusion.166 = f32[8,256,32]{1,2,0:T(8,128)S(1)} fusion(f32[8,256,32]{1,2,0:T(8,128)} %fusion.176, bf16[8,768,256]{2,1,0:T(8,128)(2,1)} %gather_fusion.12, pred[8]{0:T(512)(128)(4,1)S(1)} %get-tuple-element.56, f32[8,256]{1,0:T(8,128)S(1)} %broadcast_select_fusion.4, f32[8,256]{1,0:T(8,128)S(1)} %add.386, bf16[96,8,8,256]{3,2,1,0:T(8,128)(2,1)} %bitcast.272, ...), kind=kOutput, calls=%fused_computation.114 | convolution fusion | flops 843251712 | bytes 6963216 | tf_op jit(solution)/shard_map/pia,iab->pib/dot_general | solution.py:73
  156.7 5.0 %gather_fusion.15 = bf16[8,768,256]{2,1,0:T(8,128)(2,1)} fusion(bf16[768,14,256]{2,0,1:T(8,128)(2,1)} %copy.46, s32[1024]{0:T(1024)S(1)} %pad_clamp_fusion.7), kind=kCustom, calls=%fused_computation.11.clone | custom fusion | bytes 6291488 | tf_op jit(solution)/shard_map/jit(_take)/gather | solution.py:68
  164.2 3.9 %fusion.156 = f32[8,256,32]{1,2,0:T(8,128)S(1)} fusion(f32[8,256,32]{1,2,0:T(8,128)S(1)} %fusion.166, bf16[8,768,256]{2,1,0:T(8,128)(2,1)} %gather_fusion.15, pred[8]{0:T(512)(128)(4,1)S(1)} %get-tuple-element.55, f32[8,256]{1,0:T(8,128)S(1)} %broadcast_select_fusion.3, f32[8,256]{1,0:T(8,128)S(1)} %add.386, bf16[96,8,8,256]{3,2,1,0:T(8,128)(2,1)} %bitcast.273, ...), kind=kOutput, calls=%fused_computation.112 | convolution fusion | flops 843251712 | bytes 6963216 | tf_op jit(solution)/shard_map/pia,iab->pib/dot_general | solution.py:73
  169.2 5.0 %gather_fusion.18 = bf16[8,768,256]{2,1,0:T(8,128)(2,1)} fusion(bf16[768,14,256]{2,0,1:T(8,128)(2,1)} %copy.46, s32[1024]{0:T(1024)S(1)} %pad_clamp_fusion.6), kind=kCustom, calls=%fused_computation.12.clone | custom fusion | bytes 6291488 | tf_op jit(solution)/shard_map/jit(_take)/gather | solution.py:68
  174.3 5.2 %fusion.146 = f32[8,256,32]{1,2,0:T(8,128)} fusion(f32[8,256,32]{1,2,0:T(8,128)S(1)} %fusion.156, bf16[8,768,256]{2,1,0:T(8,128)(2,1)} %gather_fusion.18, pred[8]{0:T(512)(128)(4,1)S(1)} %get-tuple-element.54, f32[8,256]{1,0:T(8,128)S(1)} %broadcast_select_fusion.2, f32[8,256]{1,0:T(8,128)S(1)} %add.386, bf16[96,8,8,256]{3,2,1,0:T(8,128)(2,1)} %bitcast.274, ...), kind=kOutput, calls=%fused_computation.110 | convolution fusion | flops 843251712 | bytes 6963216 | tf_op jit(solution)/shard_map/pia,iab->pib/dot_general | solution.py:73
  180.7 5.0 %gather_fusion.21 = bf16[8,768,256]{2,1,0:T(8,128)(2,1)} fusion(bf16[768,14,256]{2,0,1:T(8,128)(2,1)} %copy.46, s32[1024]{0:T(1024)S(1)} %pad_clamp_fusion.5), kind=kCustom, calls=%fused_computation.13.clone | custom fusion | bytes 6291488 | tf_op jit(solution)/shard_map/jit(_take)/gather | solution.py:68
  187.5 3.9 %fusion.136 = f32[8,256,32]{1,2,0:T(8,128)S(1)} fusion(f32[8,256,32]{1,2,0:T(8,128)S(1)} %copy-done.9, bf16[8,768,256]{2,1,0:T(8,128)(2,1)} %gather_fusion.21, pred[8]{0:T(512)(128)(4,1)S(1)} %get-tuple-element.53, f32[8,256]{1,0:T(8,128)S(1)} %broadcast_select_fusion.1, f32[8,256]{1,0:T(8,128)S(1)} %add.386, bf16[96,8,8,256]{3,2,1,0:T(8,128)(2,1)} %bitcast.275, ...), kind=kOutput, calls=%fused_computation.108 | convolution fusion | flops 843251712 | bytes 6963216 | tf_op jit(solution)/shard_map/pia,iab->pib/dot_general | solution.py:73
  192.6 5.0 %gather_fusion.24 = bf16[8,768,256]{2,1,0:T(8,128)(2,1)} fusion(bf16[768,14,256]{2,0,1:T(8,128)(2,1)} %copy.46, s32[1024]{0:T(1024)S(1)} %pad_clamp_fusion.4), kind=kCustom, calls=%fused_computation.14.clone | custom fusion | bytes 6291488 | tf_op jit(solution)/shard_map/jit(_take)/gather | solution.py:68
  200.3 3.9 %fusion.126 = f32[8,4,8,256]{3,2,1,0:T(8,128)S(1)} fusion(f32[8,256,32]{1,2,0:T(8,128)S(1)} %fusion.136, bf16[8,768,256]{2,1,0:T(8,128)(2,1)} %gather_fusion.24, pred[8]{0:T(512)(128)(4,1)S(1)} %get-tuple-element.52, f32[8,256]{1,0:T(8,128)S(1)} %broadcast_select_fusion, f32[8,256]{1,0:T(8,128)S(1)} %add.386, bf16[96,8,8,256]{3,2,1,0:T(8,128)(2,1)} %bitcast.276, ...), kind=kOutput, calls=%fused_computation.106 | convolution fusion | flops 843251712 | bytes 6963216 | tf_op jit(solution)/shard_map/pia,iab->pib/dot_general | solution.py:73
  204.4 7.2 %collective-permute-done.6 = f32[32,1920]{1,0:T(8,128)S(1)} collective-permute-done((f32[32,1920]{1,0:T(8,128)S(1)}, f32[32,1920]{1,0:T(8,128)S(1)}, u32[]{:S(2)}, u32[]{:S(2)}) %collective-permute-start.6) | collective-permute-done | bytes 245792 | tf_op jit(solution)/shard_map/ppermute | solution.py:138
  212.4 3.2 %fusion.44 = f32[2048,32]{0,1:T(8,128)S(1)} fusion(f32[32,2048]{1,0:T(8,128)S(1)} %bitcast.284, bf16[768,2048]{1,0:T(8,128)(2,1)} %param.13, f32[2048]{0:T(1024)S(1)} %multiply_reduce_fusion.1, f32[256]{0:T(256)S(1)} %multiply_reduce_fusion.2, bf16[768,64]{0,1:T(8,128)(2,1)S(1)} %get-tuple-element.28, bf16[768,64]{0,1:T(8,128)(2,1)S(1)} %get-tuple-element.30, ...), kind=kOutput, calls=%fused_computation.79 | convolution fusion | flops 843186176 | bytes 4088832 | tf_op jit(solution)/shard_map/dot_general | solution.py:154
  216.0 5.8 %scatter_custom_fusion = f32[32,2048]{0,1:T(8,128)S(1)} fusion(s32[2048]{0:T(1024)S(1)} %bitcast.286, f32[2048,32]{1,0:T(8,128)S(1)} %copy.80, f32[]{:T(128)} %constant.201.clone.1), kind=kCustom, calls=%fused_computation.168 | custom fusion | bytes 262148 | tf_op jit(solution)/shard_map/scatter | solution.py:158
  (129 shorter events, 46.9 us)
Async XLA Ops:
  6.5 205.0 %copy-start = (f32[30,64,64]{2,1,0:T(8,128)S(1)}, f32[30,64,64]{2,1,0:T(8,128)}, u32[]{:S(2)}) copy-start(f32[30,64,64]{2,1,0:T(8,128)} %param.19) | copy-start | bytes 1474564
  6.5 95.9 %all-gather.3.cloned.1.call-start = ((), (), s32[]{:S(2)}) async-start(), calls=%async_computation | async-start | bytes 3244032 | tf_op jit(solution)/shard_map/all_gather | solution.py:103
  18.3 9.8 %copy-start.3 = (s32[1,2048]{1,0:T(1,128)S(1)}, s32[1,2048]{1,0:T(1,128)}, u32[]{:S(2)}) copy-start(s32[1,2048]{1,0:T(1,128)} %param.15) | copy-start | bytes 24580
  18.3 9.8 %copy-start.1 = (bf16[32,2048]{1,0:T(8,128)(2,1)S(1)}, bf16[32,2048]{1,0:T(8,128)(2,1)}, u32[]{:S(2)}) copy-start(bf16[32,2048]{1,0:T(8,128)(2,1)} %param.14) | copy-start | bytes 393220
  40.1 10.0 %copy-start.4 = (s32[1,8]{1,0:T(1,128)S(1)}, s32[1,8]{1,0:T(1,128)}, u32[]{:S(2)}) copy-start(s32[1,8]{1,0:T(1,128)} %param.17) | copy-start | bytes 100
  40.1 10.6 %collective-permute-start.1 = (bf16[800,768]{1,0:T(8,128)(2,1)}, bf16[800,768]{1,0:T(8,128)(2,1)}, u32[]{:S(2)}, u32[]{:S(2)}) collective-permute-start(bf16[800,768]{1,0:T(8,128)(2,1)} %copy.43), channel_id=1, source_target_pairs={{1,0},{2,1},{3,2},{4,3},{5,4},{6,5},{7,6},{8,7},{9,8},{10,9},{11,1... | collective-permute-start | bytes 3686408 | tf_op jit(solution)/shard_map/ppermute | solution.py:21
  43.0 9.5 %collective-permute-start = (bf16[800,768]{1,0:T(8,128)(2,1)}, bf16[800,768]{1,0:T(8,128)(2,1)}, u32[]{:S(2)}, u32[]{:S(2)}) collective-permute-start(bf16[800,768]{1,0:T(8,128)(2,1)} %copy.42), channel_id=1, source_target_pairs={{0,1},{1,2},{2,3},{3,4},{4,5},{5,6},{6,7},{7,8},{8,9},{9,10},{10,1... | collective-permute-start | bytes 3686408 | tf_op jit(solution)/shard_map/ppermute | solution.py:18
  121.6 29.4 %copy-start.2 = (bf16[8,32,256]{2,1,0:T(8,128)(2,1)S(1)}, bf16[8,32,256]{2,1,0:T(8,128)(2,1)}, u32[]{:S(2)}) copy-start(bf16[8,32,256]{2,1,0:T(8,128)(2,1)} %gather_fusion.13) | copy-start | bytes 393220
  121.6 29.4 %copy-start.8 = (pred[8]{0:T(512)(128)(4,1)S(1)}, pred[8]{0:T(512)(128)(4,1)}, u32[]{:S(2)}) copy-start(pred[8]{0:T(512)(128)(4,1)} %get-tuple-element.42) | copy-start | bytes 28
  126.5 35.2 %collective-permute-start.2 = (f32[32,1920]{1,0:T(8,128)S(1)}, f32[32,1920]{1,0:T(8,128)S(1)}, u32[]{:S(2)}, u32[]{:S(2)}) collective-permute-start(f32[32,1920]{1,0:T(8,128)S(1)} %dynamic_update_slice.15), channel_id=1, source_target_pairs={{0,1},{1,0},{2,3},{3,2},{4,5},{5,4},{6,7},{7,6},{8,9},{9,8},{10,11... | collective-permute-start | bytes 737288 | tf_op jit(solution)/shard_map/ppermute | solution.py:138
  156.7 7.5 %copy-start.7 = (pred[8]{0:T(512)(128)(4,1)S(1)}, pred[8]{0:T(512)(128)(4,1)}, u32[]{:S(2)}) copy-start(pred[8]{0:T(512)(128)(4,1)} %get-tuple-element.41) | copy-start | bytes 28
  161.7 12.5 %collective-permute-start.3 = (f32[32,1920]{1,0:T(8,128)S(1)}, f32[32,1920]{1,0:T(8,128)S(1)}, u32[]{:S(2)}, u32[]{:S(2)}) collective-permute-start(f32[32,1920]{1,0:T(8,128)S(1)} %add.440), channel_id=1, source_target_pairs={{0,2},{1,3},{2,0},{3,1},{4,6},{5,7},{6,4},{7,5},{8,10},{9,11},{10,... | collective-permute-start | bytes 737288 | tf_op jit(solution)/shard_map/ppermute | solution.py:138
  169.2 5.2 %copy-start.6 = (pred[8]{0:T(512)(128)(4,1)S(1)}, pred[8]{0:T(512)(128)(4,1)}, u32[]{:S(2)}) copy-start(pred[8]{0:T(512)(128)(4,1)} %get-tuple-element.40) | copy-start | bytes 28
  174.3 11.6 %collective-permute-start.4 = (f32[32,1920]{1,0:T(8,128)S(1)}, f32[32,1920]{1,0:T(8,128)S(1)}, u32[]{:S(2)}, u32[]{:S(2)}) collective-permute-start(f32[32,1920]{1,0:T(8,128)S(1)} %add.441), channel_id=1, source_target_pairs={{0,4},{1,5},{2,6},{3,7},{4,0},{5,1},{6,2},{7,3},{8,12},{9,13},{10,... | collective-permute-start | bytes 737288 | tf_op jit(solution)/shard_map/ppermute | solution.py:138
  180.7 6.8 %copy-start.5 = (pred[8]{0:T(512)(128)(4,1)S(1)}, pred[8]{0:T(512)(128)(4,1)}, u32[]{:S(2)}) copy-start(pred[8]{0:T(512)(128)(4,1)} %get-tuple-element.45) | copy-start | bytes 28
  180.7 6.8 %copy-start.9 = (f32[8,256,32]{1,2,0:T(8,128)S(1)}, f32[8,256,32]{1,2,0:T(8,128)}, u32[]{:S(2)}) copy-start(f32[8,256,32]{1,2,0:T(8,128)} %fusion.146) | copy-start | bytes 786436
  185.8 11.7 %collective-permute-start.5 = (f32[32,1920]{1,0:T(8,128)S(1)}, f32[32,1920]{1,0:T(8,128)S(1)}, u32[]{:S(2)}, u32[]{:S(2)}) collective-permute-start(f32[32,1920]{1,0:T(8,128)S(1)} %add.442), channel_id=1, source_target_pairs={{0,8},{1,9},{2,10},{3,11},{4,12},{5,13},{6,14},{7,15},{8,0},{9,1},... | collective-permute-start | bytes 737288 | tf_op jit(solution)/shard_map/ppermute | solution.py:138
  197.6 13.9 %collective-permute-start.6 = (f32[32,1920]{1,0:T(8,128)S(1)}, f32[32,1920]{1,0:T(8,128)S(1)}, u32[]{:S(2)}, u32[]{:S(2)}) collective-permute-start(f32[32,1920]{1,0:T(8,128)S(1)} %add.443), channel_id=1, source_target_pairs={{0,16},{1,17},{2,18},{3,19},{4,20},{5,21},{6,22},{7,23},{8,24},{9,... | collective-permute-start | bytes 737288 | tf_op jit(solution)/shard_map/ppermute | solution.py:138
Sparse Core Ops, SparseCore 0:
  28.2 68.3 all-gather.2
